TPU v7x, 32 devices: a whole 2x2x4 slice. The times are simulated.
32 devices in a mesh: fsdp: 8 (over z, y), seq: 4 (over x, core).
Axes of the slice: x: 2, y: 2, z: 4, core: 2. Of those that a mesh axis runs over, the one named last changes fastest.
Arguments:
- frames_in: bfloat16 [16, 1536, 1280], P('fsdp', 'seq'), may hold values from -6 to 6
- teacher: bfloat16 [16, 1536, 1280], P('fsdp', 'seq'), may hold values from -6 to 6
- lengths: int32 [16], replicated, may hold values from 384 to 1536, as said below
- norm1_gain: bfloat16 [1280], P('fsdp'), may hold values from 0.25 to 1.75
- norm1_bias: bfloat16 [1280], P('fsdp'), may hold values from -1.75 to 1.75
- w_qkv: bfloat16 [1280, 3840], P('fsdp'), may hold values from -0.15625 to 0.15625
- query_bias: bfloat16 [1280], P('fsdp'), may hold values from -1.75 to 1.75
- value_bias: bfloat16 [1280], P('fsdp'), may hold values from -1.75 to 1.75
- w_attn_out: bfloat16 [1280, 1280], P('fsdp'), may hold values from -0.875 to 0.875
- attn_out_bias: bfloat16 [1280], P('fsdp'), may hold values from -1.75 to 1.75
- norm2_gain: bfloat16 [1280], P('fsdp'), may hold values from 0.25 to 1.75
- norm2_bias: bfloat16 [1280], P('fsdp'), may hold values from -1.75 to 1.75
- w_up: bfloat16 [1280, 5120], P('fsdp'), may hold values from -0.15625 to 0.15625
- up_bias: bfloat16 [5120], P('fsdp'), may hold values from -1.75 to 1.75
- w_down: bfloat16 [5120, 1280], P('fsdp'), may hold values from -0.125 to 0.125
- down_bias: bfloat16 [1280], P('fsdp'), may hold values from -1.75 to 1.75
Outputs:
- frames_out: bfloat16 [16, 1536, 1280], P('fsdp', 'seq')
- clip_loss: float32 [16], P('fsdp')
- grad_in: float32 [16, 1536, 1280], P('fsdp', 'seq')
- grad_norm1_gain: float32 [1280], P('fsdp')
- grad_norm1_bias: float32 [1280], P('fsdp')
- grad_w_qkv: float32 [1280, 3840], P('fsdp')
- grad_query_bias: float32 [1280], P('fsdp')
- grad_value_bias: float32 [1280], P('fsdp')
- grad_w_attn_out: float32 [1280, 1280], P('fsdp')
- grad_attn_out_bias: float32 [1280], P('fsdp')
- grad_norm2_gain: float32 [1280], P('fsdp')
- grad_norm2_bias: float32 [1280], P('fsdp')
- grad_w_up: float32 [1280, 5120], P('fsdp')
- grad_up_bias: float32 [5120], P('fsdp')
- grad_w_down: float32 [5120, 1280], P('fsdp')
- grad_down_bias: float32 [1280], P('fsdp')
Inputs may be any that keep to these rules, and one draw needn't show every extreme that they name: `lengths`: a clip's valid frames are its first ones; in every draw some clip has all 1536 frames valid.
All inputs are finite; a program needn't handle non-finite values.
Results may differ from a plain program's by a relative error of at most 0.0095.
Values may be sent and summed in bfloat16 or wider, within the bound.
A program may use at most 256 MiB of HBM per device.

v0:
```python
import functools
import math
import jax
import jax.numpy as jnp
from jax import lax
from jax.sharding import PartitionSpec as P

HEADS = 16


def layer_norm(v, gain, bias):
    mean = jnp.mean(v, axis=-1, keepdims=True)
    cent = v - mean
    var = jnp.mean(cent * cent, axis=-1, keepdims=True)
    return cent * lax.rsqrt(var + 1e-05) * gain + bias


def local(
    frames_in,
    teacher,
    lengths,
    norm1_gain,
    norm1_bias,
    w_qkv,
    query_bias,
    value_bias,
    w_attn_out,
    attn_out_bias,
    norm2_gain,
    norm2_bias,
    w_up,
    up_bias,
    w_down,
    down_bias,
):
    single = jnp.float32
    half = jnp.bfloat16
    gain1, bias1, wqkv, qbias, vbias, wout, obias, gain2, bias2, wup, ubias, wdown, dbias = (
        lax.all_gather(norm1_gain, "fsdp", axis=0, tiled=True),
        lax.all_gather(norm1_bias, "fsdp", axis=0, tiled=True),
        lax.all_gather(w_qkv, "fsdp", axis=0, tiled=True),
        lax.all_gather(query_bias, "fsdp", axis=0, tiled=True),
        lax.all_gather(value_bias, "fsdp", axis=0, tiled=True),
        lax.all_gather(w_attn_out, "fsdp", axis=0, tiled=True),
        lax.all_gather(attn_out_bias, "fsdp", axis=0, tiled=True),
        lax.all_gather(norm2_gain, "fsdp", axis=0, tiled=True),
        lax.all_gather(norm2_bias, "fsdp", axis=0, tiled=True),
        lax.all_gather(w_up, "fsdp", axis=0, tiled=True),
        lax.all_gather(up_bias, "fsdp", axis=0, tiled=True),
        lax.all_gather(w_down, "fsdp", axis=0, tiled=True),
        lax.all_gather(down_bias, "fsdp", axis=0, tiled=True),
    )
    clips, frames, width = frames_in.shape
    groups = lax.axis_size("seq")
    seq_len = frames * groups
    head_dim = width // HEADS
    local_heads = HEADS // groups
    span = local_heads * head_dim
    rows = clips * frames
    block = min(512, seq_len)
    nblocks = seq_len // block
    scale = 1.0 / math.sqrt(head_dim)
    mine = lax.dynamic_slice_in_dim(lengths, lax.axis_index("fsdp") * clips, clips)
    place = lax.axis_index("seq") * frames + jnp.arange(frames, dtype=jnp.int32)
    row_valid = (place[None, :] < mine[:, None]).astype(single)
    key_valid = jnp.arange(seq_len, dtype=jnp.int32)[None, :] < mine[:, None]
    state = frames_in.astype(single).reshape(rows, width)
    hidden1, norm1_back = jax.vjp(layer_norm, state, gain1.astype(single), bias1.astype(single))
    hidden1 = hidden1.astype(half)
    qkv = jnp.dot(hidden1, wqkv, preferred_element_type=single)
    query = (qkv[:, :width] + qbias.astype(single)).astype(half)
    keyed = qkv[:, width : 2 * width].astype(half)
    valued = (qkv[:, 2 * width :] + vbias.astype(single)).astype(half)

    def to_groups(tensor):
        return tensor.reshape(clips, frames, groups, span)

    query_h, keyed_h, valued_h = (
        lax.all_to_all(to_groups(query), "seq", split_axis=2, concat_axis=1, tiled=True),
        lax.all_to_all(to_groups(keyed), "seq", split_axis=2, concat_axis=1, tiled=True),
        lax.all_to_all(to_groups(valued), "seq", split_axis=2, concat_axis=1, tiled=True),
    )
    query_h = query_h.reshape(clips, seq_len, local_heads, head_dim)
    keyed_h = keyed_h.reshape(clips, seq_len, local_heads, head_dim)
    valued_h = valued_h.reshape(clips, seq_len, local_heads, head_dim)

    def scores_of(query_block, keys, valid):
        scores = (
            jnp.einsum("qhd,khd->hqk", query_block, keys, preferred_element_type=single) * scale
        )
        return jnp.where(valid[None, None, :], scores, -1e30)

    def attend(item):
        queries, keys, values, valid = item
        blocks = queries.reshape(nblocks, block, local_heads, head_dim)

        def one_block(query_block):
            scores = scores_of(query_block, keys, valid)
            top = jnp.max(scores, axis=-1, keepdims=True)
            expo = jnp.exp(scores - top)
            total = jnp.sum(expo, axis=-1, keepdims=True)
            probs = (expo / total).astype(half)
            context = jnp.einsum("hqk,khd->qhd", probs, values, preferred_element_type=single)
            return (context.astype(half), (top + jnp.log(total))[..., 0])

        context, logsum = lax.map(one_block, blocks)
        return (context.reshape(seq_len, span), logsum)

    context_h, logsum = lax.map(attend, (query_h, keyed_h, valued_h, key_valid))
    context = lax.all_to_all(
        context_h.reshape(clips, seq_len, 1, span), "seq", split_axis=1, concat_axis=2, tiled=True
    ).reshape(rows, width)
    attn = jnp.dot(context, wout, preferred_element_type=single) + obias.astype(single)
    middle = state + attn
    hidden2, norm2_back = jax.vjp(layer_norm, middle, gain2.astype(single), bias2.astype(single))
    hidden2 = hidden2.astype(half)
    upper = jnp.dot(hidden2, wup, preferred_element_type=single) + ubias.astype(single)
    active, gelu_back = jax.vjp(functools.partial(jax.nn.gelu, approximate=False), upper)
    active = active.astype(half)
    result = middle + jnp.dot(active, wdown, preferred_element_type=single) + dbias.astype(single)
    frames_out = result.astype(half).reshape(clips, frames, width)
    count = jnp.sum(lengths).astype(single)
    diff = (result - teacher.astype(single).reshape(rows, width)).reshape(clips, frames, width)
    masked = diff * row_valid[:, :, None]
    part_loss = jnp.sum(masked * diff, axis=(1, 2)) / (2.0 * width * count)
    grad_out = (masked * (float(lengths.shape[0] * seq_len) / count)).reshape(rows, width)
    wqkv_b, wout_b, wup_b, wdown_b = (
        lax.all_gather(w_qkv, "fsdp", axis=0, tiled=True),
        lax.all_gather(w_attn_out, "fsdp", axis=0, tiled=True),
        lax.all_gather(w_up, "fsdp", axis=0, tiled=True),
        lax.all_gather(w_down, "fsdp", axis=0, tiled=True),
    )
    grad_branch2 = grad_out.astype(half)
    grad_wdown = jnp.dot(active.T, grad_branch2, preferred_element_type=single)
    grad_dbias = jnp.sum(grad_branch2.astype(single), axis=0)
    grad_active = jnp.dot(grad_branch2, wdown_b.T, preferred_element_type=single)
    (grad_upper,) = gelu_back(grad_active)
    grad_upper = grad_upper.astype(half)
    grad_wup = jnp.dot(hidden2.T, grad_upper, preferred_element_type=single)
    grad_ubias = jnp.sum(grad_upper.astype(single), axis=0)
    grad_hidden2 = jnp.dot(grad_upper, wup_b.T, preferred_element_type=single)
    grad_middle_norm, grad_gain2, grad_bias2 = norm2_back(grad_hidden2)
    grad_middle = grad_out + grad_middle_norm
    grad_branch1 = grad_middle.astype(half)
    grad_wout = jnp.dot(context.T, grad_branch1, preferred_element_type=single)
    grad_obias = jnp.sum(grad_branch1.astype(single), axis=0)
    grad_context = jnp.dot(grad_branch1, wout_b.T, preferred_element_type=single).astype(half)
    grad_context_h = lax.all_to_all(
        grad_context.reshape(clips, frames, groups, span),
        "seq",
        split_axis=2,
        concat_axis=1,
        tiled=True,
    )
    grad_context_h = grad_context_h.reshape(clips, seq_len, local_heads, head_dim)

    def attend_back(item):
        queries, keys, values, grads, sums, valid = item
        query_blocks = queries.reshape(nblocks, block, local_heads, head_dim)
        grad_blocks = grads.reshape(nblocks, block, local_heads, head_dim)

        def one_block(carry, piece):
            query_block, grad_block, sum_block = piece
            scores = scores_of(query_block, keys, valid)
            probs = jnp.exp(scores - sum_block[..., None])
            grad_probs = jnp.einsum(
                "qhd,khd->hqk", grad_block, values, preferred_element_type=single
            )
            inner = jnp.sum(probs * grad_probs, axis=-1, keepdims=True)
            grad_scores = (probs * (grad_probs - inner)).astype(half)
            grad_query = (
                jnp.einsum("hqk,khd->qhd", grad_scores, keys, preferred_element_type=single) * scale
            )
            grad_keys = (
                carry[0]
                + jnp.einsum(
                    "hqk,qhd->khd", grad_scores, query_block, preferred_element_type=single
                )
                * scale
            )
            grad_values = carry[1] + jnp.einsum(
                "hqk,qhd->khd", probs.astype(half), grad_block, preferred_element_type=single
            )
            return ((grad_keys, grad_values), grad_query.astype(half))

        empty = jnp.zeros((seq_len, local_heads, head_dim), single)
        (grad_keys, grad_values), grad_queries = lax.scan(
            one_block, (empty, empty), (query_blocks, grad_blocks, sums)
        )
        return (
            grad_queries.reshape(seq_len, 1, span),
            grad_keys.astype(half).reshape(seq_len, 1, span),
            grad_values.astype(half).reshape(seq_len, 1, span),
        )

    grad_query_h, grad_keyed_h, grad_valued_h = lax.map(
        attend_back, (query_h, keyed_h, valued_h, grad_context_h, logsum, key_valid)
    )
    grad_query, grad_keyed, grad_valued = (
        lax.all_to_all(grad_query_h, "seq", split_axis=1, concat_axis=2, tiled=True),
        lax.all_to_all(grad_keyed_h, "seq", split_axis=1, concat_axis=2, tiled=True),
        lax.all_to_all(grad_valued_h, "seq", split_axis=1, concat_axis=2, tiled=True),
    )
    grad_query = grad_query.reshape(rows, width)
    grad_keyed = grad_keyed.reshape(rows, width)
    grad_valued = grad_valued.reshape(rows, width)
    grad_qkv = jnp.concatenate([grad_query, grad_keyed, grad_valued], axis=1)
    grad_wqkv = jnp.dot(hidden1.T, grad_qkv, preferred_element_type=single)
    grad_qbias = jnp.sum(grad_query.astype(single), axis=0)
    grad_vbias = jnp.sum(grad_valued.astype(single), axis=0)
    grad_hidden1 = jnp.dot(grad_qkv, wqkv_b.T, preferred_element_type=single)
    grad_state_norm, grad_gain1, grad_bias1 = norm1_back(grad_hidden1)
    grad_in = (grad_middle + grad_state_norm).reshape(clips, frames, width)
    gradients = (
        grad_gain1,
        grad_bias1,
        grad_wqkv,
        grad_qbias,
        grad_vbias,
        grad_wout,
        grad_obias,
        grad_gain2,
        grad_bias2,
        grad_wup,
        grad_ubias,
        grad_wdown,
        grad_dbias,
    )
    owned = (
        lax.psum_scatter(
            gradients[0].astype(jnp.bfloat16), "fsdp", scatter_dimension=0, tiled=True
        ).astype(jnp.float32),
        lax.psum_scatter(
            gradients[1].astype(jnp.bfloat16), "fsdp", scatter_dimension=0, tiled=True
        ).astype(jnp.float32),
        lax.psum_scatter(
            gradients[2].astype(jnp.bfloat16), "fsdp", scatter_dimension=0, tiled=True
        ).astype(jnp.float32),
        lax.psum_scatter(
            gradients[3].astype(jnp.bfloat16), "fsdp", scatter_dimension=0, tiled=True
        ).astype(jnp.float32),
        lax.psum_scatter(
            gradients[4].astype(jnp.bfloat16), "fsdp", scatter_dimension=0, tiled=True
        ).astype(jnp.float32),
        lax.psum_scatter(
            gradients[5].astype(jnp.bfloat16), "fsdp", scatter_dimension=0, tiled=True
        ).astype(jnp.float32),
        lax.psum_scatter(
            gradients[6].astype(jnp.bfloat16), "fsdp", scatter_dimension=0, tiled=True
        ).astype(jnp.float32),
        lax.psum_scatter(
            gradients[7].astype(jnp.bfloat16), "fsdp", scatter_dimension=0, tiled=True
        ).astype(jnp.float32),
        lax.psum_scatter(
            gradients[8].astype(jnp.bfloat16), "fsdp", scatter_dimension=0, tiled=True
        ).astype(jnp.float32),
        lax.psum_scatter(
            gradients[9].astype(jnp.bfloat16), "fsdp", scatter_dimension=0, tiled=True
        ).astype(jnp.float32),
        lax.psum_scatter(
            gradients[10].astype(jnp.bfloat16), "fsdp", scatter_dimension=0, tiled=True
        ).astype(jnp.float32),
        lax.psum_scatter(
            gradients[11].astype(jnp.bfloat16), "fsdp", scatter_dimension=0, tiled=True
        ).astype(jnp.float32),
        lax.psum_scatter(
            gradients[12].astype(jnp.bfloat16), "fsdp", scatter_dimension=0, tiled=True
        ).astype(jnp.float32),
    )
    reduced = (
        lax.psum(owned[0].astype(jnp.bfloat16), "seq").astype(jnp.float32),
        lax.psum(owned[1].astype(jnp.bfloat16), "seq").astype(jnp.float32),
        lax.psum(owned[2].astype(jnp.bfloat16), "seq").astype(jnp.float32),
        lax.psum(owned[3].astype(jnp.bfloat16), "seq").astype(jnp.float32),
        lax.psum(owned[4].astype(jnp.bfloat16), "seq").astype(jnp.float32),
        lax.psum(owned[5].astype(jnp.bfloat16), "seq").astype(jnp.float32),
        lax.psum(owned[6].astype(jnp.bfloat16), "seq").astype(jnp.float32),
        lax.psum(owned[7].astype(jnp.bfloat16), "seq").astype(jnp.float32),
        lax.psum(owned[8].astype(jnp.bfloat16), "seq").astype(jnp.float32),
        lax.psum(owned[9].astype(jnp.bfloat16), "seq").astype(jnp.float32),
        lax.psum(owned[10].astype(jnp.bfloat16), "seq").astype(jnp.float32),
        lax.psum(owned[11].astype(jnp.bfloat16), "seq").astype(jnp.float32),
        lax.psum(owned[12].astype(jnp.bfloat16), "seq").astype(jnp.float32),
        lax.psum(part_loss.astype(jnp.bfloat16), "seq").astype(jnp.float32),
    )
    summed = tuple(reduced[:13])
    clip_loss = reduced[13]
    return (
        frames_out,
        clip_loss,
        grad_in,
        summed[0],
        summed[1],
        summed[2],
        summed[3],
        summed[4],
        summed[5],
        summed[6],
        summed[7],
        summed[8],
        summed[9],
        summed[10],
        summed[11],
        summed[12],
    )


def solution(mesh):
    placed = (
        P("fsdp", "seq", None),
        P("fsdp", "seq", None),
        P(),
        P("fsdp"),
        P("fsdp"),
        P("fsdp", None),
        P("fsdp"),
        P("fsdp"),
        P("fsdp", None),
        P("fsdp"),
        P("fsdp"),
        P("fsdp"),
        P("fsdp", None),
        P("fsdp"),
        P("fsdp", None),
        P("fsdp"),
    )
    return jax.shard_map(
        local,
        mesh=mesh,
        in_specs=placed,
        out_specs=(
            P("fsdp", "seq", None),
            P("fsdp"),
            P("fsdp", "seq", None),
            P("fsdp"),
            P("fsdp"),
            P("fsdp", None),
            P("fsdp"),
            P("fsdp"),
            P("fsdp", None),
            P("fsdp"),
            P("fsdp"),
            P("fsdp"),
            P("fsdp", None),
            P("fsdp"),
            P("fsdp", None),
            P("fsdp"),
        ),
        check_vma=False,
    )
```

profile of v0, /device:TPU:0, one launch (start us, length us, event | category | flops | bytes accessed | tf_op | source)
XLA Modules:
  0.0 1777.0 jit_solution(1138143871130389060)
XLA Ops:
  18.2 41.9 %all-reduce.18 = (bf16[1280]{0:T(1024)(128)(2,1)S(1)}, bf16[1280]{0:T(1024)(128)(2,1)S(1)}, bf16[1280]{0:T(1024)(128)(2,1)S(1)}, bf16[1280]{0:T(1024)(128)(2,1)S...) all-reduce(bf16[1280]{0:T(1024)(128)(2,1)S(1)} %dynamic-update-slic, ...), channel_id=1, replica_groups=mesh['fsdp'=8,'seq'=4] {'fsdp'}, use_global_device_ids=true, to_apply=%add.1 | all-reduce | flops 10240 | bytes 40960
  63.8 92.2 %all-gather.6.cloned.1.call-done = bf16[1280,3840]{1,0:T(8,128)(2,1)} async-done(((bf16[160,3840]{1,0:T(8,128)(2,1)}), bf16[1280,3840]{1,0:T(8,128)(2,1)}) %all-gather.6.cloned.1.call-update) | async-done | bytes 9830416 | tf_op jit(solution)/shard_map/all_gather | solution.py:41
  156.0 10.7 fusion.73
  194.7 15.3 all-to-all-done
  226.9 11.8 all-to-all-done.2
  260.4 6.1 all-to-all-done.1
  273.6 70.0 %while.54 = (s32[]{:T(128)}, bf16[2,1536,320]{1,2,0:T(8,128)(2,1)}, f32[2,3,4,512]{3,2,1,0:T(4,128)S(1)}, bf16[2,1536,4,80]{1,3,2,0:T(8,128)(2,1)}, bf16[2,1536,...) while((s32[]{:T(128)}, bf16[2,1536,320]{1,2,0:T(8,128)(2,1)}, ...), condition=%wide.region_7.8_spmd, body=%wide.region_2.7_spmd.sunk | while | flops 1044543488 | bytes 64087352 | solution.py:109
  277.6 27.9 %while.57 = (s32[]{:T(128)}, bf16[3,512,4,80]{1,3,2,0:T(8,128)(2,1)S(1)}, f32[3,4,512]{2,1,0:T(4,128)S(1)}, pred[1536]{0:T(1024)(128)(4,1)S(1)}, bf16[3,512,4,80...) while((s32[]{:T(128)}, ...), condition=%wide.region_6.6_spmd, body=%wide.region_3.5_spmd.sunk | while | flops 1044543488 | bytes 40441440 | solution.py:106
  312.5 27.8 %while.57 = (s32[]{:T(128)}, bf16[3,512,4,80]{1,3,2,0:T(8,128)(2,1)S(1)}, f32[3,4,512]{2,1,0:T(4,128)S(1)}, pred[1536]{0:T(1024)(128)(4,1)S(1)}, bf16[3,512,4,80...) while((s32[]{:T(128)}, ...), condition=%wide.region_6.6_spmd, body=%wide.region_3.5_spmd.sunk | while | flops 1044543488 | bytes 40441440 | solution.py:106
  343.7 6.8 copy.181
  354.8 31.4 %all-gather = bf16[8,1,640]{2,1,0:T(2,128)(2,1)S(1)} all-gather(bf16[1,1,640]{2,1,0:T(2,128)(2,1)S(1)} %reshape.315), channel_id=1, replica_groups=mesh['fsdp'=8,'seq'=4] {'fsdp'}, dimensions={0}, use_global_device_ids=true | all-gather | bytes 11520 | tf_op jit(solution)/shard_map/all_gather | solution.py:49
  388.5 8.7 copy.182
  408.8 51.7 %multiply_convert_fusion.1 = (bf16[768,5120]{1,0:T(8,128)(2,1)}, f32[768,5120]{1,0:T(8,128)}, f32[768,5120]{1,0:T(8,128)}) fusion(f32[5120]{0:T(1024)S(1)} %bitcast.260, bf16[1280,5120]{1,0:T(8,128)(2,1)} %all-gather.10.cloned.1.call-done, f32[768,1280]{1,0:T(8,128)} %copy-done.6, f32[1280]{0:T(1024)S(1)} %convert_element_type.214, ...), kind=kOutput, calls=%fused_computation.64 | convolution fusion | flops 10330767360 | bytes 56397824 | tf_op jit(solution)/shard_map/dot_general | solution.py:117
  460.5 123.9 %all-gather.12.cloned.1.call-done = bf16[5120,1280]{1,0:T(8,128)(2,1)} async-done(((bf16[640,1280]{1,0:T(8,128)(2,1)}), bf16[5120,1280]{1,0:T(8,128)(2,1)}) %all-gather.12.cloned.1.call-update) | async-done | bytes 13107216 | tf_op jit(solution)/shard_map/all_gather | solution.py:50
  584.3 18.9 %fusion.45 = (f32[768]{0:T(1024)}, bf16[768,1280]{1,0:T(8,128)(2,1)}, f32[768,1280]{1,0:T(8,128)S(1)}) fusion(f32[768]{0:T(1024)S(1)} %compare_convert_fusion, bf16[2,384,1280]{2,1,0:T(8,128)(2,1)S(1)} %copy-done.16, f32[1280]{0:T(1024)S(1)} %convert_element_type.218, f32[768,1280]{1,0:T(8,128)} %copy-done.6, bf16[768,5120]{1,0:T(8,128)(2,1)} %get-tuple-element.481, ...), kind=kOutput, calls=%fused_computation.86 | convolution fusion | flops 10074192896 | bytes 32779264 | tf_op jit(solution)/shard_map/dot_general | solution.py:120
  606.3 24.6 %fusion.68 = (bf16[5120]{0:T(1024)(128)(2,1)}, bf16[768,5120]{1,0:T(8,128)(2,1)}) fusion(f32[768,5120]{1,0:T(8,128)} %get-tuple-element.482, f32[768,5120]{1,0:T(8,128)} %get-tuple-element.501, f32[5120]{0:T(1024)S(1)} %bitcast.261, bf16[768,1280]{1,0:T(8,128)(2,1)} %get-tuple-element.474, bf16[5120,1280]{1,0:T(8,128)(2,1)} %all-gather.12.cloned.1.call-done), kind=kOutput, calls=%fused_computation.142 | convolution fusion | flops 10129239040 | bytes 54425600 | tf_op jit(solution)/shard_map/dot_general | solution.py:136
  630.9 19.5 %multiply_reduce_fusion.1 = (bf16[1280]{0:T(1024)(128)(2,1)}, f32[768]{0:T(1024)S(1)}, bf16[1280]{0:T(1024)(128)(2,1)}, f32[768,1280]{1,0:T(8,128)}) fusion(f32[768,1280]{1,0:T(8,128)} %copy-done.6, f32[768]{0:T(1024)S(1)} %fusion.60, f32[768]{0:T(1024)S(1)} %broadcast_multiply_fusion, f32[1280]{0:T(1024)S(1)} %convert_element_type.213, ...), kind=kOutput, calls=%fused_computation.108 | convolution fusion | flops 10074190848 | bytes 28855296 | tf_op jit(solution)/shard_map/dot_general | solution.py:141
  674.4 24.2 %all-to-all-done.4 = bf16[2,384,4,320]{1,0,3,2:T(2,128)(2,1)S(1)} async-done(((bf16[2,384,4,320]{1,0,3,2:T(2,128)(2,1)}), bf16[2,384,4,320]{1,0,3,2:T(2,128)(2,1)S(1)}, u32[]{:S(2)}, u32[]{:S(2)}) %all-to-all-start.4) | async-done | bytes 1966112 | tf_op jit(solution)/shard_map/all_to_all | solution.py:148
  705.6 227.1 %while.56 = (s32[]{:T(128)}, bf16[2,1536,1,320]{1,3,2,0:T(8,128)(2,1)}, bf16[2,1536,1,320]{1,3,2,0:T(8,128)(2,1)}, bf16[2,1536,1,320]{1,3,2,0:T(8,128)(2,1)}, bf...) while((s32[]{:T(128)}, ...), condition=%wide.region_20.21_spmd, body=%wide.region_16.20_spmd.sunk | while | flops 2548660224 | bytes 254784048 | solution.py:196
  714.5 93.9 %while.58 = (s32[]{:T(128)}, f32[1536,4,80]{0,2,1:T(8,128)S(1)}, f32[1536,4,80]{0,2,1:T(8,128)}, bf16[3,512,4,80]{1,3,2,0:T(8,128)(2,1)}, bf16[3,512,4,80]{1,3,2...) while((s32[]{:T(128)}, f32[1536,4,80]{0,2,1:T(8,128)S(1)}, ...), condition=%wide.region_19.19_spmd.clone, body=%wide.region_17.18_spmd.clone.sunk | while | flops 2547677184 | bytes 207532240 | solution.py:187
  735.3 6.5 fusion.131
  766.1 6.5 fusion.131
  797.6 6.5 fusion.131
  828.0 93.9 %while.58 = (s32[]{:T(128)}, f32[1536,4,80]{0,2,1:T(8,128)S(1)}, f32[1536,4,80]{0,2,1:T(8,128)}, bf16[3,512,4,80]{1,3,2,0:T(8,128)(2,1)}, bf16[3,512,4,80]{1,3,2...) while((s32[]{:T(128)}, f32[1536,4,80]{0,2,1:T(8,128)S(1)}, ...), condition=%wide.region_19.19_spmd.clone, body=%wide.region_17.18_spmd.clone.sunk | while | flops 2547677184 | bytes 207532240 | solution.py:187
  848.8 6.5 fusion.131
  879.7 6.5 fusion.131
  911.2 6.5 fusion.131
  932.7 6.7 copy.185
  943.1 7.1 convolution_convert_fusion.3
  950.3 6.7 copy.188
  957.0 14.5 all-to-all-done.5
  976.0 6.8 copy.191
  982.8 21.7 %all-to-all-done.6 = bf16[2,1536,1,320]{3,0,2,1:T(2,128)(2,1)} async-done(((bf16[2,1536,1,320]{3,0,2,1:T(2,128)(2,1)}), bf16[2,1536,1,320]{3,0,2,1:T(2,128)(2,1)}, u32[]{:S(2)}, u32[]{:S(2)}) %all-to-all-start.6) | async-done | bytes 1966112 | tf_op jit(solution)/shard_map/all_to_all | solution.py:201
  1009.6 6.6 copy.200
  1019.9 6.6 copy.201
  1030.2 7.5 all-to-all-done.7
  1037.6 6.6 copy.202
  1050.7 10.1 convolution_convert_fusion.2
  1061.5 17.3 convolution_convert_fusion.1
  1080.3 16.3 convolution_convert_fusion
  1098.6 15.0 fusion.65
  1113.5 114.4 %reduce-scatter.5.cloned.1.call-done = bf16[160,3840]{1,0:T(8,128)(2,1)} async-done(((bf16[1280,3840]{1,0:T(8,128)(2,1)}), bf16[160,3840]{1,0:T(8,128)(2,1)}) %reduce-scatter.5.cloned.1.call-update) | async-done | bytes 1228816 | tf_op jit(solution)/shard_map/reduce_scatter | solution.py:236
  1227.9 217.4 %reduce-scatter.9.cloned.1.call-done = bf16[160,5120]{1,0:T(8,128)(2,1)} async-done(((bf16[1280,5120]{1,0:T(8,128)(2,1)}), bf16[160,5120]{1,0:T(8,128)(2,1)}) %reduce-scatter.9.cloned.1.call-update) | async-done | bytes 1638416 | tf_op jit(solution)/shard_map/reduce_scatter | solution.py:257
  1445.3 217.5 %reduce-scatter.11.cloned.1.call-done = bf16[640,1280]{1,0:T(8,128)(2,1)} async-done(((bf16[5120,1280]{1,0:T(8,128)(2,1)}), bf16[640,1280]{1,0:T(8,128)(2,1)}) %reduce-scatter.11.cloned.1.call-update) | async-done | bytes 1638416 | tf_op jit(solution)/shard_map/reduce_scatter | solution.py:263
  1671.7 35.7 %all-reduce.17 = (bf16[1280]{0:T(1024)(128)(2,1)S(1)}, bf16[1280]{0:T(1024)(128)(2,1)S(1)}, bf16[1280]{0:T(1024)(128)(2,1)S(1)}, bf16[1280]{0:T(1024)(128)(2,1)S...) all-reduce(bf16[1280]{0:T(1024)(128)(2,1)S(1)} %get-tuple-element.3, ...), channel_id=2, replica_groups=mesh['fsdp'=8,'seq'=4] {'fsdp'}, use_global_device_ids=true, to_apply=%region_24.25.clone | all-reduce | flops 15360 | bytes 61440
  1708.1 5.7 all-reduce.19
  1719.5 6.2 add_add_fusion.2
  1725.6 36.5 %all-reduce.23.cloned.1.call-done = (bf16[160,3840]{1,0:T(8,128)(2,1)}, bf16[160,1280]{1,0:T(8,128)(2,1)}, bf16[160,5120]{1,0:T(8,128)(2,1)}, bf16[640,1280]{1,0:T(8,128)(2,1)}) async-done(((bf16[160,3840]{1,0:T(8,128)(2,1)}, bf16[160,1280]{1,0:T(8,128)(2,1)}, bf16[160,5120]{1,0:T(8,128)(2,1)}, bf16[640,1280]{1,0:T(8,128)(2,1)}), (bf16[160,3840]{1,0:T(8,128)(2,1)}, bf16[160,1280]{1,0:T(8,128)(2,1)}, ...) | async-done | bytes 4915216 | tf_op jit(solution)/shard_map/psum | solution.py:273
  (430 shorter events, 448.6 us)
Async XLA Ops:
  7.2 52.9 %copy-start.2 = (bf16[2,384,1280]{2,1,0:T(8,128)(2,1)S(1)}, bf16[2,384,1280]{2,1,0:T(8,128)(2,1)}, u32[]{:S(2)}) copy-start(bf16[2,384,1280]{2,1,0:T(8,128)(2,1)} %param.24) | copy-start | bytes 5898244
  7.2 148.8 %all-gather.6.cloned.1.call-start = ((), (), s32[]{:S(2)}) async-start(), calls=%async_computation.12 | async-start | bytes 11059200 | tf_op jit(solution)/shard_map/all_gather | solution.py:41
  7.9 392.6 %all-gather.8.cloned.1.call-start = ((), (), s32[]{:S(2)}) async-start(), calls=%async_computation.13 | async-start | bytes 3686400 | tf_op jit(solution)/shard_map/all_gather | solution.py:44
  8.7 400.1 %all-gather.10.cloned.1.call-start = ((), (), s32[]{:S(2)}) async-start(), calls=%async_computation.14 | async-start | bytes 14745600 | tf_op jit(solution)/shard_map/all_gather | solution.py:48
  60.5 106.3 %copy-start.35 = (f32[768]{0:T(1024)}, f32[768]{0:T(1024)S(1)}, u32[]{:S(2)}) copy-start(f32[768]{0:T(1024)S(1)} %div.56) | copy-start | bytes 9220
  61.1 105.6 %copy-start.41 = (f32[768]{0:T(1024)}, f32[768]{0:T(1024)S(1)}, u32[]{:S(2)}) copy-start(f32[768]{0:T(1024)S(1)} %add.192) | copy-start | bytes 9220
  181.2 28.7 %all-to-all-start = ((bf16[2,384,4,320]{1,0,3,2:T(2,128)(2,1)}), bf16[2,384,4,320]{1,0,3,2:T(2,128)(2,1)}, u32[]{:S(2)}, u32[]{:S(2)}) async-start(bf16[2,384,4,320]{1,0,3,2:T(2,128)(2,1)} %copy.196), calls=%async_computation | async-start | bytes 3932160 | tf_op jit(solution)/shard_map/all_to_all | solution.py:79
  209.9 28.7 %all-to-all-start.2 = ((bf16[2,384,4,320]{1,0,3,2:T(2,128)(2,1)}), bf16[2,384,4,320]{1,0,3,2:T(2,128)(2,1)}, u32[]{:S(2)}, u32[]{:S(2)}) async-start(bf16[2,384,4,320]{1,0,3,2:T(2,128)(2,1)} %copy.198), calls=%async_computation.2 | async-start | bytes 3932160 | tf_op jit(solution)/shard_map/all_to_all | solution.py:81
  222.0 20.9 %copy-start.64 = (s32[16]{0:T(128)S(1)}, s32[16]{0:T(128)}, u32[]{:S(2)}) copy-start(s32[16]{0:T(128)} %param.26) | copy-start | bytes 196
  238.7 27.8 %all-to-all-start.1 = ((bf16[2,384,4,320]{1,0,3,2:T(2,128)(2,1)}), bf16[2,384,4,320]{1,0,3,2:T(2,128)(2,1)S(1)}, u32[]{:S(2)}, u32[]{:S(2)}) async-start(bf16[2,384,4,320]{1,0,3,2:T(2,128)(2,1)} %copy.197), calls=%async_computation.1 | async-start | bytes 3932160 | tf_op jit(solution)/shard_map/all_to_all | solution.py:80
  242.3 342.0 %all-gather.12.cloned.1.call-start = ((), (), s32[]{:S(2)}) async-start(), calls=%async_computation.15 | async-start | bytes 14745600 | tf_op jit(solution)/shard_map/all_gather | solution.py:50
  243.0 8.7 copy-start.62
  343.6 6.8 copy-start.27
  343.6 6.8 copy-start.32
  343.6 10.5 copy-start.65
  343.6 11.1 copy-start.57
  343.6 11.1 copy-start.56
  343.6 11.1 copy-start.55
  343.6 11.1 copy-start.61
  343.7 42.6 %copy-start.54 = (bf16[1280]{0:T(1024)(128)(2,1)S(1)}, bf16[1280]{0:T(1024)(128)(2,1)}, u32[]{:S(2)}) copy-start(bf16[1280]{0:T(1024)(128)(2,1)} %get-tuple-element.458) | copy-start | bytes 7684
  343.7 42.6 %copy-start.63 = (s32[2]{0:T(128)S(1)}, s32[2]{0:T(128)}, u32[]{:S(2)}) copy-start(s32[2]{0:T(128)} %copy-done.62) | copy-start | bytes 28
  350.4 36.7 %all-to-all-start.3 = ((bf16[2,1536,1,320]{3,0,2,1:T(2,128)(2,1)}), bf16[2,1536,1,320]{3,0,2,1:T(2,128)(2,1)S(1)}, u32[]{:S(2)}, u32[]{:S(2)}) async-start(bf16[2,1536,1,320]{3,0,2,1:T(2,128)(2,1)} %bitcast.245), calls=%async_computation.3 | async-start | bytes 4718592 | tf_op jit(solution)/shard_map/all_to_all | solution.py:110
  354.7 295.7 %copy-start.45 = (f32[1280]{0:T(1024)}, f32[1280]{0:T(1024)S(1)}, u32[]{:S(2)}) copy-start(f32[1280]{0:T(1024)S(1)} %convert_element_type.213) | copy-start | bytes 15364
  354.8 54.0 %copy-start.52 = (f32[1280]{0:T(1024)}, f32[1280]{0:T(1024)S(1)}, u32[]{:S(2)}) copy-start(f32[1280]{0:T(1024)S(1)} %convert_element_type.214) | copy-start | bytes 15364
  388.5 12.0 copy-start.3
  406.2 244.2 %copy-start.39 = (f32[768]{0:T(1024)}, f32[768]{0:T(1024)S(1)}, u32[]{:S(2)}) copy-start(f32[768]{0:T(1024)S(1)} %broadcast_multiply_fusion) | copy-start | bytes 9220
  408.7 51.8 %copy-start.43 = (f32[768]{0:T(1024)}, f32[768]{0:T(1024)S(1)}, u32[]{:S(2)}) copy-start(f32[768]{0:T(1024)S(1)} %multiply_reduce_fusion.3) | copy-start | bytes 9220
  408.7 241.7 %copy-start.47 = (f32[768]{0:T(1024)}, f32[768]{0:T(1024)S(1)}, u32[]{:S(2)}) copy-start(f32[768]{0:T(1024)S(1)} %fusion.60) | copy-start | bytes 9220
  408.7 175.6 %copy-start.16 = (bf16[2,384,1280]{2,1,0:T(8,128)(2,1)S(1)}, bf16[2,384,1280]{2,1,0:T(8,128)(2,1)}, u32[]{:S(2)}) copy-start(bf16[2,384,1280]{2,1,0:T(8,128)(2,1)} %param.25) | copy-start | bytes 5898244
  630.9 19.5 %copy-start.44 = (f32[768]{0:T(1024)S(1)}, f32[768]{0:T(1024)}, u32[]{:S(2)}) copy-start(f32[768]{0:T(1024)} %copy-done.43) | copy-start | bytes 9220
  630.9 19.6 %copy-start.7 = (f32[768,1280]{1,0:T(8,128)S(1)}, f32[768,1280]{1,0:T(8,128)}, u32[]{:S(2)}) copy-start(f32[768,1280]{1,0:T(8,128)} %copy-done.6) | copy-start | bytes 11796484
  670.7 27.8 %all-to-all-start.4 = ((bf16[2,384,4,320]{1,0,3,2:T(2,128)(2,1)}), bf16[2,384,4,320]{1,0,3,2:T(2,128)(2,1)S(1)}, u32[]{:S(2)}, u32[]{:S(2)}) async-start(bf16[2,384,4,320]{1,0,3,2:T(2,128)(2,1)} %copy.199), calls=%async_computation.4 | async-start | bytes 3932160 | tf_op jit(solution)/shard_map/all_to_all | solution.py:148
  698.6 7.0 copy-start.28
  730.9 10.9 copy-start.1
  761.8 10.9 copy-start.1
  793.3 10.9 copy-start.1
  844.5 10.9 copy-start.1
  875.3 10.9 copy-start.1
  906.9 10.9 copy-start.1
  939.4 32.1 %all-to-all-start.5 = ((bf16[2,1536,1,320]{3,0,2,1:T(2,128)(2,1)}), bf16[2,1536,1,320]{3,0,2,1:T(2,128)(2,1)S(1)}, u32[]{:S(2)}, u32[]{:S(2)}) async-start(bf16[2,1536,1,320]{3,0,2,1:T(2,128)(2,1)} %copy.185), calls=%async_computation.5 | async-start | bytes 4718592 | tf_op jit(solution)/shard_map/all_to_all | solution.py:200
  943.1 170.4 %reduce-scatter.7.cloned.1.call-start = ((), (), s32[]{:S(2)}) async-start(), calls=%async_computation.17 | async-start | bytes 3686400 | tf_op jit(solution)/shard_map/reduce_scatter | solution.py:245
  971.5 11.3 copy-start.14
  971.5 33.0 %all-to-all-start.6 = ((bf16[2,1536,1,320]{3,0,2,1:T(2,128)(2,1)}), bf16[2,1536,1,320]{3,0,2,1:T(2,128)(2,1)}, u32[]{:S(2)}, u32[]{:S(2)}) async-start(bf16[2,1536,1,320]{3,0,2,1:T(2,128)(2,1)} %copy.188), calls=%async_computation.6 | async-start | bytes 4718592 | tf_op jit(solution)/shard_map/all_to_all | solution.py:201
  1004.6 33.1 %all-to-all-start.7 = ((bf16[2,1536,1,320]{3,0,2,1:T(2,128)(2,1)}), bf16[2,1536,1,320]{3,0,2,1:T(2,128)(2,1)}, u32[]{:S(2)}, u32[]{:S(2)}) async-start(bf16[2,1536,1,320]{3,0,2,1:T(2,128)(2,1)} %copy.191), calls=%async_computation.7 | async-start | bytes 4718592 | tf_op jit(solution)/shard_map/all_to_all | solution.py:202
  1009.1 218.8 %reduce-scatter.5.cloned.1.call-start = ((), (), s32[]{:S(2)}) async-start(), calls=%async_computation.16 | async-start | bytes 11059200 | tf_op jit(solution)/shard_map/reduce_scatter | solution.py:236
  1060.8 384.5 %reduce-scatter.9.cloned.1.call-start = ((), (), s32[]{:S(2)}) async-start(), calls=%async_computation.18 | async-start | bytes 14745600 | tf_op jit(solution)/shard_map/reduce_scatter | solution.py:257
  1078.8 584.0 %reduce-scatter.11.cloned.1.call-start = ((), (), s32[]{:S(2)}) async-start(), calls=%async_computation.19 | async-start | bytes 14745600 | tf_op jit(solution)/shard_map/reduce_scatter | solution.py:263
  1096.7 665.4 %all-reduce.23.cloned.1.call-start = ((), (), s32[]{:S(2)}) async-start(), calls=%async_computation.20 | async-start | bytes 9830400 | tf_op jit(solution)/shard_map/psum | solution.py:273
  (49 other events, 159.3 us)
Sparse Core Ops, SparseCore 0:
  10.2 145.8 all-gather.5
  158.2 59.6 all-gather.7
  220.1 181.2 all-gather.9
  403.4 180.8 all-gather.11
  950.4 74.5 reduce-scatter.6
  1060.9 166.9 reduce-scatter.4
  1231.5 213.7 reduce-scatter.8
  1449.0 213.8 reduce-scatter.10
  1665.4 96.6 all-reduce.22
where the time goes:
time: 1790 us; the launch traced here: 1780 us
  waiting for transfers between devices  905 us (51%)
  matrix products  379 us (21%)
  local copies, waits for them, and re-layouts  240 us (13%)
  blocking collectives  115 us (6%)
  other arithmetic  85 us (5%)
  starting transfers between devices  34 us (2%)
    reduce_scatter x1, waiting for transfers between devices, local(): lax.psum_scatter(gradients[11].astype(jnp.bfloat16), 'fsdp', scatter_dime...  217 us
    reduce_scatter x1, waiting for transfers between devices, local(): lax.psum_scatter(gradients[9].astype(jnp.bfloat16), 'fsdp', scatter_dimen...  217 us
    all_gather x1, waiting for transfers between devices, local(): lax.all_gather(w_down, 'fsdp', axis=0, tiled=True)  124 us
    reduce_scatter x1, waiting for transfers between devices, local(): lax.psum_scatter(gradients[2].astype(jnp.bfloat16), 'fsdp', scatter_dimen...  114 us
    all_gather x1, waiting for transfers between devices, local(): lax.all_gather(w_qkv, 'fsdp', axis=0, tiled=True)  92.2 us
    unnamed x2, blocking collectives  77.6 us
    dot_general x1, matrix products, local(): jnp.dot(hidden2, wup, preferred_element_type=single) + ubias.astype(single)  51.7 us
    dot_general x12, matrix products, scores_of(): jnp.einsum('qhd,khd->hqk', query_block, keys, preferred_element_type=single)  45.4 us
  transfers between devices with their start and end apart: 17, of which 13 were waited for; matrix products, arithmetic and copies ran while one was open for 20% of the time, Pallas kernels for 0%

commit v1 on v0

--- a/solution.py
+++ b/solution.py
@@ -270,7 +270,7 @@
     reduced = (
         lax.psum(owned[0].astype(jnp.bfloat16), "seq").astype(jnp.float32),
         lax.psum(owned[1].astype(jnp.bfloat16), "seq").astype(jnp.float32),
-        lax.psum(owned[2].astype(jnp.bfloat16), "seq").astype(jnp.float32),
+        jnp.sum(lax.all_gather(owned[2].astype(jnp.bfloat16), "seq"), axis=0).astype(jnp.float32),
         lax.psum(owned[3].astype(jnp.bfloat16), "seq").astype(jnp.float32),
         lax.psum(owned[4].astype(jnp.bfloat16), "seq").astype(jnp.float32),
         lax.psum(owned[5].astype(jnp.bfloat16), "seq").astype(jnp.float32),

time: 1790 us -> 1490 us (0.83)
  waiting for transfers between devices: 905 us -> 599 us
    reduce_scatter x1, waiting for transfers between devices: 217 us -> 0.02 us  [local(): lax.psum_scatter(gradients[9].astype(jnp.bfloat16), 'fsdp', scatter_dimen...]
    reduce_scatter x1, waiting for transfers between devices: 217 us -> 82.2 us  [local(): lax.psum_scatter(gradients[11].astype(jnp.bfloat16), 'fsdp', scatter_dime...]
    reduce_scatter x1, waiting for transfers between devices: 114 us -> 172 us  [local(): lax.psum_scatter(gradients[2].astype(jnp.bfloat16), 'fsdp', scatter_dimen...]
    psum x1, waiting for transfers between devices: 36.5 us -> 0.37 us  [local(): lax.psum(owned[5].astype(jnp.bfloat16), 'seq').astype(jnp.float32)]
    all_gather x0 -> x1, waiting for transfers between devices: none -> 33.5 us  [local(): lax.all_gather(owned[2].astype(jnp.bfloat16), 'seq')]
  transfers between devices with their start and end apart: 17 -> 18, of which waited for: 13 -> 13; matrix products, arithmetic and copies ran while one was open for 20% -> 39% of each run, Pallas kernels for 0% -> 0%
where the time goes in v1:
time: 1490 us; the launch traced here: 1480 us
  waiting for transfers between devices  599 us (40%)
  matrix products  378 us (25%)
  local copies, waits for them, and re-layouts  244 us (16%)
  blocking collectives  116 us (8%)
  other arithmetic  85.6 us (6%)
  starting transfers between devices  33.4 us (2%)
  between operations  18 us (1%)
    reduce_scatter x1, waiting for transfers between devices, local(): lax.psum_scatter(gradients[2].astype(jnp.bfloat16), 'fsdp', scatter_dimen...  172 us
    all_gather x1, waiting for transfers between devices, local(): lax.all_gather(w_down, 'fsdp', axis=0, tiled=True)  124 us
    all_gather x1, waiting for transfers between devices, local(): lax.all_gather(w_qkv, 'fsdp', axis=0, tiled=True)  92.2 us
    reduce_scatter x1, waiting for transfers between devices, local(): lax.psum_scatter(gradients[11].astype(jnp.bfloat16), 'fsdp', scatter_dime...  82.2 us
    unnamed x2, blocking collectives  78 us
    dot_general x1, matrix products, local(): jnp.dot(hidden2, wup, preferred_element_type=single) + ubias.astype(single)  51.6 us
    dot_general x12, matrix products, scores_of(): jnp.einsum('qhd,khd->hqk', query_block, keys, preferred_element_type=single)  45.4 us
    dot_general x6, matrix products, one_block(): jnp.einsum('hqk,khd->qhd', grad_scores, keys, preferred_element_type=single)  39.5 us
  transfers between devices with their start and end apart: 18, of which 13 were waited for; matrix products, arithmetic and copies ran while one was open for 39% of the time, Pallas kernels for 0%

profile of v1, /device:TPU:0, one launch (start us, length us, event | category | flops | bytes accessed | tf_op | source)
XLA Modules:
  0.0 1475.1 jit_solution(9564663880637217557)
XLA Ops:
  18.2 41.9 %all-reduce.18 = (bf16[1280]{0:T(1024)(128)(2,1)S(1)}, bf16[1280]{0:T(1024)(128)(2,1)S(1)}, bf16[1280]{0:T(1024)(128)(2,1)S(1)}, bf16[1280]{0:T(1024)(128)(2,1)S...) all-reduce(bf16[1280]{0:T(1024)(128)(2,1)S(1)} %dynamic-update-slic, ...), channel_id=1, replica_groups=mesh['fsdp'=8,'seq'=4] {'fsdp'}, use_global_device_ids=true, to_apply=%add.1 | all-reduce | flops 10240 | bytes 40960
  63.9 92.2 %all-gather.8.cloned.1.call-done = bf16[1280,3840]{1,0:T(8,128)(2,1)} async-done(((bf16[160,3840]{1,0:T(8,128)(2,1)}), bf16[1280,3840]{1,0:T(8,128)(2,1)}) %all-gather.8.cloned.1.call-update) | async-done | bytes 9830416 | tf_op jit(solution)/shard_map/all_gather | solution.py:41
  156.0 10.8 fusion.73
  194.8 15.3 %all-to-all-done = bf16[2,384,4,320]{1,0,3,2:T(2,128)(2,1)} async-done(((bf16[2,384,4,320]{1,0,3,2:T(2,128)(2,1)}), bf16[2,384,4,320]{1,0,3,2:T(2,128)(2,1)}, u32[]{:S(2)}, u32[]{:S(2)}) %all-to-all-start) | async-done | bytes 1966112 | tf_op jit(solution)/shard_map/all_to_all | solution.py:79
  227.0 11.8 all-to-all-done.2
  260.4 6.2 all-to-all-done.1
  273.7 70.0 %while.54 = (s32[]{:T(128)}, bf16[2,1536,320]{1,2,0:T(8,128)(2,1)}, f32[2,3,4,512]{3,2,1,0:T(4,128)S(1)}, bf16[2,1536,4,80]{1,3,2,0:T(8,128)(2,1)}, bf16[2,1536,...) while((s32[]{:T(128)}, bf16[2,1536,320]{1,2,0:T(8,128)(2,1)}, ...), condition=%wide.region_7.8_spmd, body=%wide.region_2.7_spmd.sunk | while | flops 1044543488 | bytes 64087352 | solution.py:109
  277.7 27.9 %while.57 = (s32[]{:T(128)}, bf16[3,512,4,80]{1,3,2,0:T(8,128)(2,1)S(1)}, f32[3,4,512]{2,1,0:T(4,128)S(1)}, pred[1536]{0:T(1024)(128)(4,1)S(1)}, bf16[3,512,4,80...) while((s32[]{:T(128)}, ...), condition=%wide.region_6.6_spmd, body=%wide.region_3.5_spmd.sunk | while | flops 1044543488 | bytes 40441440 | solution.py:106
  312.7 27.8 %while.57 = (s32[]{:T(128)}, bf16[3,512,4,80]{1,3,2,0:T(8,128)(2,1)S(1)}, f32[3,4,512]{2,1,0:T(4,128)S(1)}, pred[1536]{0:T(1024)(128)(4,1)S(1)}, bf16[3,512,4,80...) while((s32[]{:T(128)}, ...), condition=%wide.region_6.6_spmd, body=%wide.region_3.5_spmd.sunk | while | flops 1044543488 | bytes 40441440 | solution.py:106
  343.9 6.8 copy.181
  355.0 31.4 %all-gather.1 = bf16[8,1,640]{2,1,0:T(2,128)(2,1)S(1)} all-gather(bf16[1,1,640]{2,1,0:T(2,128)(2,1)S(1)} %reshape.316), channel_id=1, replica_groups=mesh['fsdp'=8,'seq'=4] {'fsdp'}, dimensions={0}, use_global_device_ids=true | all-gather | bytes 11520 | tf_op jit(solution)/shard_map/all_gather | solution.py:49
  388.8 8.7 copy.182
  400.7 5.7 fusion.72
  408.9 51.6 %multiply_convert_fusion.1 = (bf16[768,5120]{1,0:T(8,128)(2,1)}, f32[768,5120]{1,0:T(8,128)}, f32[768,5120]{1,0:T(8,128)}) fusion(f32[5120]{0:T(1024)S(1)} %bitcast.262, bf16[1280,5120]{1,0:T(8,128)(2,1)} %all-gather.12.cloned.1.call-done, f32[768,1280]{1,0:T(8,128)} %copy-done.6, f32[1280]{0:T(1024)S(1)} %convert_element_type.216, ...), kind=kOutput, calls=%fused_computation.64 | convolution fusion | flops 10330767360 | bytes 56397824 | tf_op jit(solution)/shard_map/dot_general | solution.py:117
  460.5 123.8 %all-gather.14.cloned.1.call-done = bf16[5120,1280]{1,0:T(8,128)(2,1)} async-done(((bf16[640,1280]{1,0:T(8,128)(2,1)}), bf16[5120,1280]{1,0:T(8,128)(2,1)}) %all-gather.14.cloned.1.call-update) | async-done | bytes 13107216 | tf_op jit(solution)/shard_map/all_gather | solution.py:50
  584.3 18.8 %fusion.45 = (f32[768]{0:T(1024)}, bf16[768,1280]{1,0:T(8,128)(2,1)}, f32[768,1280]{1,0:T(8,128)S(1)}) fusion(f32[768]{0:T(1024)S(1)} %compare_convert_fusion, bf16[2,384,1280]{2,1,0:T(8,128)(2,1)S(1)} %copy-done.18, f32[1280]{0:T(1024)S(1)} %convert_element_type.220, f32[768,1280]{1,0:T(8,128)} %copy-done.6, bf16[768,5120]{1,0:T(8,128)(2,1)} %get-tuple-element.480, ...), kind=kOutput, calls=%fused_computation.86 | convolution fusion | flops 10074192896 | bytes 32779264 | tf_op jit(solution)/shard_map/dot_general | solution.py:120
  606.3 24.6 %fusion.68 = (bf16[5120]{0:T(1024)(128)(2,1)}, bf16[768,5120]{1,0:T(8,128)(2,1)}) fusion(f32[768,5120]{1,0:T(8,128)} %get-tuple-element.481, f32[768,5120]{1,0:T(8,128)} %get-tuple-element.500, f32[5120]{0:T(1024)S(1)} %bitcast.263, bf16[768,1280]{1,0:T(8,128)(2,1)} %get-tuple-element.473, bf16[5120,1280]{1,0:T(8,128)(2,1)} %all-gather.14.cloned.1.call-done), kind=kOutput, calls=%fused_computation.142 | convolution fusion | flops 10129239040 | bytes 54425600 | tf_op jit(solution)/shard_map/dot_general | solution.py:136
  630.9 19.5 %multiply_reduce_fusion.1 = (bf16[1280]{0:T(1024)(128)(2,1)}, f32[768]{0:T(1024)S(1)}, bf16[1280]{0:T(1024)(128)(2,1)}, f32[768,1280]{1,0:T(8,128)}) fusion(f32[768,1280]{1,0:T(8,128)} %copy-done.6, f32[768]{0:T(1024)S(1)} %fusion.60, f32[768]{0:T(1024)S(1)} %broadcast_multiply_fusion, f32[1280]{0:T(1024)S(1)} %convert_element_type.215, ...), kind=kOutput, calls=%fused_computation.108 | convolution fusion | flops 10074190848 | bytes 28855296 | tf_op jit(solution)/shard_map/dot_general | solution.py:141
  662.0 17.3 %convolution_convert_fusion.1 = bf16[1280,5120]{1,0:T(8,128)(2,1)} fusion(bf16[768,5120]{1,0:T(8,128)(2,1)} %get-tuple-element.475, f32[768,1280]{1,0:T(8,128)} %copy-done.6, f32[1280]{0:T(1024)S(1)} %convert_element_type.216, f32[1280]{0:T(1024)S(1)} %convert_element_type.215, f32[768]{0:T(1024)S(1)} %fusion.60, f32[768]{0:T(1024)S(1)} %broadcast_multiply_fusion), kind=kOutput, calls=%fused_computation.61 | convolution fusion | flops 10077798400 | bytes 24920064 | tf_op jit(solution)/shard_map/dot_general | solution.py:139
  681.3 6.2 convolution_convert_fusion.4
  700.1 16.4 %convolution_convert_fusion = bf16[5120,1280]{1,0:T(8,128)(2,1)} fusion(bf16[768,5120]{1,0:T(8,128)(2,1)} %get-tuple-element.480, bf16[768,1280]{1,0:T(8,128)(2,1)} %get-tuple-element.473), kind=kOutput, calls=%fused_computation.60 | convolution fusion | flops 10072883200 | bytes 22937600 | tf_op jit(solution)/shard_map/dot_general | solution.py:134
  716.5 7.7 all-to-all-done.4
  731.3 229.4 %while.56 = (s32[]{:T(128)}, bf16[2,1536,1,320]{1,3,2,0:T(8,128)(2,1)}, bf16[2,1536,1,320]{1,3,2,0:T(8,128)(2,1)}, bf16[2,1536,1,320]{1,3,2,0:T(8,128)(2,1)}, bf...) while((s32[]{:T(128)}, ...), condition=%wide.region_20.21_spmd, body=%wide.region_16.20_spmd.sunk | while | flops 2548660224 | bytes 254784048 | solution.py:196
  740.6 94.6 %while.58 = (s32[]{:T(128)}, f32[1536,4,80]{0,2,1:T(8,128)S(1)}, f32[1536,4,80]{0,2,1:T(8,128)}, bf16[3,512,4,80]{1,3,2,0:T(8,128)(2,1)}, bf16[3,512,4,80]{1,3,2...) while((s32[]{:T(128)}, f32[1536,4,80]{0,2,1:T(8,128)S(1)}, ...), condition=%wide.region_19.19_spmd.clone, body=%wide.region_17.18_spmd.clone.sunk | while | flops 2547677184 | bytes 207532240 | solution.py:187
  743.4 5.5 multiply_reduce_fusion.5
  761.4 6.5 fusion.131
  792.3 6.7 fusion.131
  824.3 6.6 fusion.131
  855.0 95.0 %while.58 = (s32[]{:T(128)}, f32[1536,4,80]{0,2,1:T(8,128)S(1)}, f32[1536,4,80]{0,2,1:T(8,128)}, bf16[3,512,4,80]{1,3,2,0:T(8,128)(2,1)}, bf16[3,512,4,80]{1,3,2...) while((s32[]{:T(128)}, f32[1536,4,80]{0,2,1:T(8,128)S(1)}, ...), condition=%wide.region_19.19_spmd.clone, body=%wide.region_17.18_spmd.clone.sunk | while | flops 2547677184 | bytes 207532240 | solution.py:187
  875.9 6.5 fusion.131
  907.5 6.6 fusion.131
  939.2 6.6 fusion.131
  960.7 6.8 copy.185
  971.2 6.7 copy.188
  977.9 21.7 %all-to-all-done.5 = bf16[2,1536,1,320]{3,0,2,1:T(2,128)(2,1)S(1)} async-done(((bf16[2,1536,1,320]{3,0,2,1:T(2,128)(2,1)}), bf16[2,1536,1,320]{3,0,2,1:T(2,128)(2,1)S(1)}, u32[]{:S(2)}, u32[]{:S(2)}) %all-to-all-start.5) | async-done | bytes 1966112 | tf_op jit(solution)/shard_map/all_to_all | solution.py:200
  1004.2 6.8 copy.191
  1010.9 21.8 %all-to-all-done.6 = bf16[2,1536,1,320]{3,0,2,1:T(2,128)(2,1)} async-done(((bf16[2,1536,1,320]{3,0,2,1:T(2,128)(2,1)}), bf16[2,1536,1,320]{3,0,2,1:T(2,128)(2,1)}, u32[]{:S(2)}, u32[]{:S(2)}) %all-to-all-start.6) | async-done | bytes 1966112 | tf_op jit(solution)/shard_map/all_to_all | solution.py:201
  1037.3 6.8 copy.200
  1047.7 6.6 copy.201
  1058.1 7.7 all-to-all-done.7
  1065.7 6.6 copy.202
  1078.9 10.1 convolution_convert_fusion.2
  1089.1 82.2 %reduce-scatter.11.cloned.1.call-done = bf16[640,1280]{1,0:T(8,128)(2,1)} async-done(((bf16[5120,1280]{1,0:T(8,128)(2,1)}), bf16[640,1280]{1,0:T(8,128)(2,1)}) %reduce-scatter.11.cloned.1.call-update) | async-done | bytes 1638416 | tf_op jit(solution)/shard_map/reduce_scatter | solution.py:263
  1171.6 172.2 %reduce-scatter.5.cloned.1.call-done = bf16[160,3840]{1,0:T(8,128)(2,1)} async-done(((bf16[1280,3840]{1,0:T(8,128)(2,1)}), bf16[160,3840]{1,0:T(8,128)(2,1)}) %reduce-scatter.5.cloned.1.call-update) | async-done | bytes 1228816 | tf_op jit(solution)/shard_map/reduce_scatter | solution.py:236
  1350.6 13.7 fusion.65
  1368.3 36.1 %all-reduce.17 = (bf16[1280]{0:T(1024)(128)(2,1)S(1)}, bf16[1280]{0:T(1024)(128)(2,1)S(1)}, bf16[1280]{0:T(1024)(128)(2,1)S(1)}, bf16[1280]{0:T(1024)(128)(2,1)S...) all-reduce(bf16[1280]{0:T(1024)(128)(2,1)S(1)} %get-tuple-element.3, ...), channel_id=3, replica_groups=mesh['fsdp'=8,'seq'=4] {'fsdp'}, use_global_device_ids=true, to_apply=%region_24.25.clone | all-reduce | flops 15360 | bytes 61440
  1405.1 6.7 all-reduce.19
  1429.7 33.5 %all-gather.16.cloned.1.call-done = bf16[640,3840]{1,0:T(8,128)(2,1)} async-done(((bf16[160,3840]{1,0:T(8,128)(2,1)}), bf16[640,3840]{1,0:T(8,128)(2,1)}) %all-gather.16.cloned.1.call-update) | async-done | bytes 4915216 | tf_op jit(solution)/shard_map/all_gather | solution.py:273
  (418 shorter events, 448.0 us)
Async XLA Ops:
  7.2 52.9 %copy-start.2 = (bf16[2,384,1280]{2,1,0:T(8,128)(2,1)S(1)}, bf16[2,384,1280]{2,1,0:T(8,128)(2,1)}, u32[]{:S(2)}) copy-start(bf16[2,384,1280]{2,1,0:T(8,128)(2,1)} %param.24) | copy-start | bytes 5898244
  7.2 148.8 %all-gather.8.cloned.1.call-start = ((), (), s32[]{:S(2)}) async-start(), calls=%async_computation.12 | async-start | bytes 11059200 | tf_op jit(solution)/shard_map/all_gather | solution.py:41
  7.9 392.8 %all-gather.10.cloned.1.call-start = ((), (), s32[]{:S(2)}) async-start(), calls=%async_computation.13 | async-start | bytes 3686400 | tf_op jit(solution)/shard_map/all_gather | solution.py:44
  8.7 400.2 %all-gather.12.cloned.1.call-start = ((), (), s32[]{:S(2)}) async-start(), calls=%async_computation.14 | async-start | bytes 14745600 | tf_op jit(solution)/shard_map/all_gather | solution.py:48
  60.5 106.4 %copy-start.35 = (f32[768]{0:T(1024)}, f32[768]{0:T(1024)S(1)}, u32[]{:S(2)}) copy-start(f32[768]{0:T(1024)S(1)} %div.56) | copy-start | bytes 9220
  61.1 105.7 %copy-start.39 = (f32[768]{0:T(1024)}, f32[768]{0:T(1024)S(1)}, u32[]{:S(2)}) copy-start(f32[768]{0:T(1024)S(1)} %add.190) | copy-start | bytes 9220
  181.3 28.8 %all-to-all-start = ((bf16[2,384,4,320]{1,0,3,2:T(2,128)(2,1)}), bf16[2,384,4,320]{1,0,3,2:T(2,128)(2,1)}, u32[]{:S(2)}, u32[]{:S(2)}) async-start(bf16[2,384,4,320]{1,0,3,2:T(2,128)(2,1)} %copy.196), calls=%async_computation | async-start | bytes 3932160 | tf_op jit(solution)/shard_map/all_to_all | solution.py:79
  210.0 28.8 %all-to-all-start.2 = ((bf16[2,384,4,320]{1,0,3,2:T(2,128)(2,1)}), bf16[2,384,4,320]{1,0,3,2:T(2,128)(2,1)}, u32[]{:S(2)}, u32[]{:S(2)}) async-start(bf16[2,384,4,320]{1,0,3,2:T(2,128)(2,1)} %copy.198), calls=%async_computation.2 | async-start | bytes 3932160 | tf_op jit(solution)/shard_map/all_to_all | solution.py:81
  222.1 20.9 %copy-start.56 = (s32[16]{0:T(128)S(1)}, s32[16]{0:T(128)}, u32[]{:S(2)}) copy-start(s32[16]{0:T(128)} %param.26) | copy-start | bytes 196
  238.8 27.8 %all-to-all-start.1 = ((bf16[2,384,4,320]{1,0,3,2:T(2,128)(2,1)}), bf16[2,384,4,320]{1,0,3,2:T(2,128)(2,1)S(1)}, u32[]{:S(2)}, u32[]{:S(2)}) async-start(bf16[2,384,4,320]{1,0,3,2:T(2,128)(2,1)} %copy.197), calls=%async_computation.1 | async-start | bytes 3932160 | tf_op jit(solution)/shard_map/all_to_all | solution.py:80
  242.4 341.9 %all-gather.14.cloned.1.call-start = ((), (), s32[]{:S(2)}) async-start(), calls=%async_computation.15 | async-start | bytes 14745600 | tf_op jit(solution)/shard_map/all_gather | solution.py:50
  243.1 8.7 copy-start.54
  343.8 10.5 copy-start.57
  343.8 11.2 copy-start.49
  343.8 11.2 copy-start.48
  343.8 11.2 copy-start.47
  343.8 11.2 copy-start.53
  343.8 42.6 %copy-start.46 = (bf16[1280]{0:T(1024)(128)(2,1)S(1)}, bf16[1280]{0:T(1024)(128)(2,1)}, u32[]{:S(2)}) copy-start(bf16[1280]{0:T(1024)(128)(2,1)} %get-tuple-element.458) | copy-start | bytes 7684
  343.8 42.7 %copy-start.55 = (s32[2]{0:T(128)S(1)}, s32[2]{0:T(128)}, u32[]{:S(2)}) copy-start(s32[2]{0:T(128)} %copy-done.54) | copy-start | bytes 28
  350.6 36.7 %all-to-all-start.3 = ((bf16[2,1536,1,320]{3,0,2,1:T(2,128)(2,1)}), bf16[2,1536,1,320]{3,0,2,1:T(2,128)(2,1)S(1)}, u32[]{:S(2)}, u32[]{:S(2)}) async-start(bf16[2,1536,1,320]{3,0,2,1:T(2,128)(2,1)} %bitcast.246), calls=%async_computation.3 | async-start | bytes 4718592 | tf_op jit(solution)/shard_map/all_to_all | solution.py:110
  354.3 734.8 %reduce-scatter.7.cloned.1.call-start = ((), (), s32[]{:S(2)}) async-start(), calls=%async_computation.17 | async-start | bytes 3686400 | tf_op jit(solution)/shard_map/reduce_scatter | solution.py:245
  388.8 11.9 copy-start.3
  408.8 51.7 %copy-start.41 = (f32[768]{0:T(1024)}, f32[768]{0:T(1024)S(1)}, u32[]{:S(2)}) copy-start(f32[768]{0:T(1024)S(1)} %multiply_reduce_fusion.3) | copy-start | bytes 9220
  408.9 175.4 %copy-start.18 = (bf16[2,384,1280]{2,1,0:T(8,128)(2,1)S(1)}, bf16[2,384,1280]{2,1,0:T(8,128)(2,1)}, u32[]{:S(2)}) copy-start(bf16[2,384,1280]{2,1,0:T(8,128)(2,1)} %param.25) | copy-start | bytes 5898244
  630.9 19.5 %copy-start.42 = (f32[768]{0:T(1024)S(1)}, f32[768]{0:T(1024)}, u32[]{:S(2)}) copy-start(f32[768]{0:T(1024)} %copy-done.41) | copy-start | bytes 9220
  630.9 19.5 %copy-start.7 = (f32[768,1280]{1,0:T(8,128)S(1)}, f32[768,1280]{1,0:T(8,128)}, u32[]{:S(2)}) copy-start(f32[768,1280]{1,0:T(8,128)} %copy-done.6) | copy-start | bytes 11796484
  662.0 427.1 %reduce-scatter.9.cloned.1.call-start = ((), (), s32[]{:S(2)}) async-start(), calls=%async_computation.18 | async-start | bytes 14745600 | tf_op jit(solution)/shard_map/reduce_scatter | solution.py:257
  696.4 27.8 %all-to-all-start.4 = ((bf16[2,384,4,320]{1,0,3,2:T(2,128)(2,1)}), bf16[2,384,4,320]{1,0,3,2:T(2,128)(2,1)S(1)}, u32[]{:S(2)}, u32[]{:S(2)}) async-start(bf16[2,384,4,320]{1,0,3,2:T(2,128)(2,1)} %copy.199), calls=%async_computation.4 | async-start | bytes 3932160 | tf_op jit(solution)/shard_map/all_to_all | solution.py:148
  700.0 471.3 %reduce-scatter.11.cloned.1.call-start = ((), (), s32[]{:S(2)}) async-start(), calls=%async_computation.19 | async-start | bytes 14745600 | tf_op jit(solution)/shard_map/reduce_scatter | solution.py:263
  757.1 10.9 copy-start.1
  787.9 11.1 copy-start.1
  819.9 11.0 copy-start.1
  871.5 10.8 copy-start.1
  903.1 10.9 copy-start.1
  934.8 11.0 copy-start.1
  967.5 32.1 %all-to-all-start.5 = ((bf16[2,1536,1,320]{3,0,2,1:T(2,128)(2,1)}), bf16[2,1536,1,320]{3,0,2,1:T(2,128)(2,1)S(1)}, u32[]{:S(2)}, u32[]{:S(2)}) async-start(bf16[2,1536,1,320]{3,0,2,1:T(2,128)(2,1)} %copy.185), calls=%async_computation.5 | async-start | bytes 4718592 | tf_op jit(solution)/shard_map/all_to_all | solution.py:200
  999.6 11.3 copy-start.15
  999.6 33.1 %all-to-all-start.6 = ((bf16[2,1536,1,320]{3,0,2,1:T(2,128)(2,1)}), bf16[2,1536,1,320]{3,0,2,1:T(2,128)(2,1)}, u32[]{:S(2)}, u32[]{:S(2)}) async-start(bf16[2,1536,1,320]{3,0,2,1:T(2,128)(2,1)} %copy.188), calls=%async_computation.6 | async-start | bytes 4718592 | tf_op jit(solution)/shard_map/all_to_all | solution.py:201
  1032.7 33.1 %all-to-all-start.7 = ((bf16[2,1536,1,320]{3,0,2,1:T(2,128)(2,1)}), bf16[2,1536,1,320]{3,0,2,1:T(2,128)(2,1)}, u32[]{:S(2)}, u32[]{:S(2)}) async-start(bf16[2,1536,1,320]{3,0,2,1:T(2,128)(2,1)} %copy.191), calls=%async_computation.7 | async-start | bytes 4718592 | tf_op jit(solution)/shard_map/all_to_all | solution.py:202
  1037.2 306.6 %reduce-scatter.5.cloned.1.call-start = ((), (), s32[]{:S(2)}) async-start(), calls=%async_computation.16 | async-start | bytes 11059200 | tf_op jit(solution)/shard_map/reduce_scatter | solution.py:236
  1089.0 256.1 %copy-start.50 = (f32[768]{0:T(1024)S(1)}, f32[768]{0:T(1024)}, u32[]{:S(2)}) copy-start(f32[768]{0:T(1024)} %get-tuple-element.494) | copy-start | bytes 9220
  1089.0 334.1 %all-reduce.23.cloned.1.call-start = ((), (), s32[]{:S(2)}) async-start(), calls=%async_computation.21 | async-start | bytes 7372800 | tf_op jit(solution)/shard_map/psum | solution.py:276
  1171.4 179.2 %copy-start.4 = (bf16[2,384,1280]{2,1,0:T(8,128)(2,1)S(1)}, bf16[2,384,1280]{2,1,0:T(8,128)(2,1)}, u32[]{:S(2)}) copy-start(bf16[2,384,1280]{2,1,0:T(8,128)(2,1)} %param.24) | copy-start | bytes 5898244
  1171.4 179.2 %copy-start.34 = (f32[1280]{0:T(1024)S(1)}, f32[1280]{0:T(1024)}, u32[]{:S(2)}) copy-start(f32[1280]{0:T(1024)} %copy-done.33) | copy-start | bytes 15364
  1171.4 179.2 %copy-start.36 = (f32[768]{0:T(1024)S(1)}, f32[768]{0:T(1024)}, u32[]{:S(2)}) copy-start(f32[768]{0:T(1024)} %copy-done.35) | copy-start | bytes 9220
  1171.4 291.8 %all-gather.16.cloned.1.call-start = ((), (), s32[]{:S(2)}) async-start(), calls=%async_computation.20 | async-start | bytes 6144000 | tf_op jit(solution)/shard_map/all_gather | solution.py:273
  1350.6 13.8 copy-start.40
  1350.6 15.7 %copy-start.38 = (f32[768]{0:T(1024)S(1)}, f32[768]{0:T(1024)}, u32[]{:S(2)}) copy-start(f32[768]{0:T(1024)} %copy-done.37) | copy-start | bytes 9220
  (42 other events, 147.8 us)
Sparse Core Ops, SparseCore 0:
  10.2 145.8 all-gather.7
  158.2 59.6 all-gather.9
  220.1 181.2 all-gather.11
  403.4 180.8 all-gather.13
  662.1 74.4 reduce-scatter.6
  740.1 213.6 reduce-scatter.8
  957.5 213.8 reduce-scatter.10
  1175.0 168.8 reduce-scatter.4
  1346.4 76.7 all-reduce.22
  1424.6 38.5 all-gather.15
